TPU v7x, 32 devices: a whole 2x2x4 slice. The times are simulated.
32 devices in a mesh: row: 8 (over z, x), col: 4 (over y, core).
Axes of the slice: x: 2, y: 2, z: 4, core: 2. Of those that a mesh axis runs over, the one named last changes fastest.
Arguments:
- trailing: float32 [8192, 1536], P('row', 'col'), may hold values from -6 to 6
- reflectors: float32 [8192, 256], P('row', 'col'), may hold values from -6 to 6
- factor: float32 [256, 256], replicated, as said below
- column_sums: float32 [8192, 8], P('row', 'col'), may hold values from -6 to 6
- row_sums: float32 [16, 1536], P('row', 'col'), may hold values from -6 to 6
Outputs:
- updated: float32 [8192, 1536], P('row', 'col')
- column_checks: float32 [8192, 8], P('row', 'col')
- row_checks: float32 [16, 1536], P('row', 'col')
Inputs may be any that keep to these rules, and one draw needn't show every extreme that they name: `factor`: zero below the diagonal.
All inputs are finite; a program needn't handle non-finite values.
Results may differ from a plain program's by a relative error of at most 0.000067.
Values sent between devices are 32-bit elements; how exact they have to be, the bound alone decides.
No kernel may reach another device: no remote copies, remote signals or barrier semaphores. Data moves between devices by JAX's collectives and lax.ppermute only.
A program may use at most 64 MiB of HBM per device.

v0:
```python
import jax
import jax.numpy as jnp
from jax import lax
from jax.sharding import PartitionSpec as P


def matmul(left, right):
    return jnp.dot(left, right, precision=lax.Precision.HIGHEST, preferred_element_type=jnp.float32)


def shards(trailing, reflectors, factor, column_sums, row_sums):
    panel = lax.all_gather(reflectors, "col", axis=1, tiled=True)
    columns = trailing.shape[1]
    joined = jnp.concatenate([trailing, column_sums], axis=1)
    product = matmul(panel.T, joined)
    product_main = product[:, :columns]
    product_check = product[:, columns:]
    summed_main, summed_check = lax.psum((product_main, product_check), "row")
    main_image = matmul(factor.T, summed_main)
    check_image = matmul(factor.T, summed_check)
    updated = trailing - matmul(panel, main_image)
    column_checks = column_sums - matmul(panel, check_image)
    count = trailing.shape[0]
    local = jnp.arange(count).astype(jnp.float32)
    scale = 1.0 / jnp.sqrt(jnp.float32(count))
    weights = jnp.stack([jnp.ones((count,), jnp.float32) * scale, (local + 1.0) * scale / count])
    check_coeff = matmul(weights, panel)
    row_checks = row_sums - matmul(check_coeff, main_image)
    return (updated, column_checks, row_checks)


def solution(mesh):
    placed = (P("row", "col"), P("row", "col"), P(), P("row", "col"), P("row", "col"))
    return jax.shard_map(
        shards,
        mesh=mesh,
        in_specs=placed,
        out_specs=(P("row", "col"), P("row", "col"), P("row", "col")),
        check_vma=False,
    )
```

profile of v0, /device:TPU:0, one launch (start us, length us, event | category | flops | bytes accessed | tf_op | source)
XLA Modules:
  0.0 139.2 jit_solution(17977182560160107712)
XLA Ops:
  7.2 0.0 copy-start
  7.2 0.0 all-gather.2.cloned.1.call-start
  7.2 0.7 all-gather.2.cloned.1.call-update
  7.9 0.0 all-reduce.3.cloned.1.call-start
  8.0 0.9 copy.8
  8.9 0.0 copy-start.2
  8.9 3.1 %copy.9 = f32[1024,384]{0,1:T(8,128)} copy(f32[1024,384]{1,0:T(8,128)} %param.5) | data formatting | bytes 3145728 | tf_op args[0]
  12.0 17.0 %all-gather.2.cloned.1.call-done = f32[1024,256]{0,1:T(8,128)} async-done(((f32[1024,64]{0,1:T(8,128)}), f32[1024,256]{0,1:T(8,128)}) %all-gather.2.cloned.1.call-update) | async-done | bytes 1048592 | tf_op jit(solution)/shard_map/all_gather | solution.py:12
  29.0 0.0 copy-done.2
  29.0 0.0 copy-start.1
  29.0 4.7 %fusion.4 = f32[256,386]{0,1:T(8,128)S(1)} fusion(f32[1024,256]{0,1:T(8,128)} %all-gather.2.cloned.1.call-done, f32[1024,2]{1,0:T(8,128)S(1)} %copy.8, f32[1024,384]{1,0:T(8,128)S(1)} %copy-done.2), kind=kOutput, calls=%fused_computation.5 | convolution fusion | flops 1214646272 | bytes 3024896 | tf_op jit(solution)/shard_map/dot_general | solution.py:8
  33.8 0.0 copy-start.4
  33.8 0.8 slice.8
  34.5 21.3 %psum.15 = f32[256,2]{0,1:T(2,128)S(1)} all-reduce(f32[256,2]{0,1:T(2,128)S(1)} %slice.9), channel_id=1, replica_groups=mesh['row'=8,'col'=4] {'row'}, use_global_device_ids=true, to_apply=%region_1.0 | all-reduce | flops 512 | bytes 4096 | tf_op jit(solution)/shard_map/psum | solution.py:18
  55.9 0.0 all-reduce.3.cloned.1.call-update
  55.9 0.0 copy-done.1
  55.9 0.0 copy-start.3
  55.9 0.9 fusion.8
  56.8 0.0 copy-done
  56.8 0.2 fusion.13
  57.0 0.0 copy-done.4
  57.1 1.2 fusion.7
  58.3 65.9 %all-reduce.3.cloned.1.call-done = f32[256,384]{0,1:T(8,128)} async-done(((f32[256,384]{0,1:T(8,128)}), f32[256,384]{0,1:T(8,128)}) %all-reduce.3.cloned.1.call-update) | async-done | bytes 393232 | tf_op jit(solution)/shard_map/psum | solution.py:18
  124.2 1.5 %fusion.12 = f32[384,256]{1,0:T(8,128)S(1)} fusion(f32[256,384]{0,1:T(8,128)} %all-reduce.3.cloned.1.call-done, f32[256,256]{1,0:T(8,128)S(1)} %copy-done), kind=kOutput, calls=%fused_computation.14 | convolution fusion | flops 301989888 | bytes 1048576 | tf_op jit(solution)/shard_map/dot_general | solution.py:8
  125.7 0.0 copy-done.3
  125.7 2.6 %bitcast_subtract_fusion = f32[1024,384]{0,1:T(8,128)} fusion(f32[1024,384]{0,1:T(8,128)S(1)} %copy-done.3, f32[384,256]{1,0:T(8,128)S(1)} %fusion.12, f32[1024,256]{0,1:T(8,128)S(1)} %copy-done.1), kind=kOutput, calls=%fused_computation.4 | convolution fusion | flops 1208352768 | bytes 4587520 | tf_op jit(solution)/shard_map/dot_general | solution.py:8
  128.3 0.0 copy-start.5
  128.3 3.0 %copy.10 = f32[1024,384]{1,0:T(8,128)} copy(f32[1024,384]{0,1:T(8,128)} %bitcast_subtract_fusion) | data formatting | bytes 3145728
  131.4 0.0 copy-done.5
  131.4 1.0 convolution_subtract_fusion
  (2 shorter events, 0.0 us)
Async XLA Ops:
  7.2 49.7 %copy-start = (f32[256,256]{1,0:T(8,128)S(1)}, f32[256,256]{1,0:T(8,128)}, u32[]{:S(2)}) copy-start(f32[256,256]{1,0:T(8,128)} %param.7) | copy-start | bytes 786436
  7.2 21.8 %all-gather.2.cloned.1.call-start = ((), (), s32[]{:S(2)}) async-start(), calls=%async_computation | async-start | bytes 1310720 | tf_op jit(solution)/shard_map/all_gather | solution.py:12
  7.9 116.3 %all-reduce.3.cloned.1.call-start = ((), (), s32[]{:S(2)}) async-start(), calls=%async_computation.1 | async-start | bytes 786432 | tf_op jit(solution)/shard_map/psum | solution.py:18
  8.9 20.1 %copy-start.2 = (f32[1024,384]{1,0:T(8,128)S(1)}, f32[1024,384]{1,0:T(8,128)}, u32[]{:S(2)}) copy-start(f32[1024,384]{1,0:T(8,128)} %param.5) | copy-start | bytes 4718596
  29.0 26.9 %copy-start.1 = (f32[1024,256]{0,1:T(8,128)S(1)}, f32[1024,256]{0,1:T(8,128)}, u32[]{:S(2)}) copy-start(f32[1024,256]{0,1:T(8,128)} %all-gather.2.cloned.1.call-done) | copy-start | bytes 3145732
  33.8 23.3 %copy-start.4 = (f32[1024,2]{0,1:T(2,128)S(1)}, f32[1024,2]{0,1:T(2,128)}, u32[]{:S(2)}) copy-start(f32[1024,2]{0,1:T(2,128)} %param.8) | copy-start | bytes 24580
  55.9 69.8 %copy-start.3 = (f32[1024,384]{0,1:T(8,128)S(1)}, f32[1024,384]{0,1:T(8,128)}, u32[]{:S(2)}) copy-start(f32[1024,384]{0,1:T(8,128)} %copy.9) | copy-start | bytes 4718596
  128.3 3.0 %copy-start.5 = (f32[2,384]{1,0:T(2,128)S(1)}, f32[2,384]{1,0:T(2,128)}, u32[]{:S(2)}) copy-start(f32[2,384]{1,0:T(2,128)} %param.9) | copy-start | bytes 9220
Sparse Core Ops, SparseCore 0:
  9.5 19.4 all-gather.1
  56.0 68.1 all-reduce.2
where the time goes:
time: 139 us
  waiting for transfers between devices  83.6 us (60%)
  blocking collectives  21.3 us (15%)
  between operations  14.1 us (10%)
  matrix products  12.2 us (9%)
  local copies, waits for them, and re-layouts  7.89 us (6%)
    psum x1, waiting for transfers between devices, shards(): summed_main, summed_check = lax.psum((product_main, product_check), 'row')  65.9 us
    psum x1, blocking collectives, shards(): summed_main, summed_check = lax.psum((product_main, product_check), 'row')  21.3 us
    all_gather x1, waiting for transfers between devices, shards(): panel = lax.all_gather(reflectors, 'col', axis=1, tiled=True)  17 us
    dot_general x7, matrix products, matmul(): jnp.dot(left, right, precision=lax.Precision.HIGHEST, preferred_element_t...  12.2 us
    unnamed x15, local copies, waits for them, and re-layouts  7.12 us
  transfers between devices with their start and end apart: 2, of which 2 were waited for; matrix products, arithmetic and copies ran while one was open for 5% of the time, Pallas kernels for 0%

commit v1 on v0

--- a/solution.py
+++ b/solution.py
@@ -2,6 +2,18 @@
 import jax.numpy as jnp
 from jax import lax
 from jax.sharding import PartitionSpec as P
+
+
+def gather_around(array, axis, dim):
+    ways, here, hop = (lax.axis_size(axis), lax.axis_index(axis), array.shape[dim])
+    shape = [n * ways if d == dim else n for d, n in enumerate(array.shape)]
+    full = lax.dynamic_update_slice_in_dim(
+        jnp.zeros(shape, array.dtype), array, here * hop, axis=dim
+    )
+    for far in range(1, ways):
+        array = lax.ppermute(array, axis, [(d, (d + 1) % ways) for d in range(ways)])
+        full = lax.dynamic_update_slice_in_dim(full, array, (here - far) % ways * hop, axis=dim)
+    return full
 
 
 def matmul(left, right):
@@ -9,7 +21,7 @@
 
 
 def shards(trailing, reflectors, factor, column_sums, row_sums):
-    panel = lax.all_gather(reflectors, "col", axis=1, tiled=True)
+    panel = gather_around(reflectors, "col", 1)
     columns = trailing.shape[1]
     joined = jnp.concatenate([trailing, column_sums], axis=1)
     product = matmul(panel.T, joined)

time: 139 us -> 121 us (0.87)
  waiting for transfers between devices: 83.6 us -> 63.8 us
    all_gather x1 -> x0, waiting for transfers between devices: 17 us -> none  [shards(): panel = lax.all_gather(reflectors, 'col', axis=1, tiled=True)]
    psum x1, waiting for transfers between devices: 65.9 us -> 49.1 us  [shards(): summed_main, summed_check = lax.psum((product_main, product_check), 'row')]
    ppermute x0 -> x3, waiting for transfers between devices: none -> 14.7 us  [gather_around(): lax.ppermute(array, axis, [(d, (d + 1) % ways) for d in range(ways)])]
    unnamed x15 -> x13, local copies, waits for them, and re-layouts: 7.12 us -> 0.99 us
    dynamic_update_slice x0 -> x4, local copies, waits for them, and re-layouts: none -> 4.01 us  [the longest x3 2.92 us: gather_around(): lax.dynamic_update_slice_in_dim(full, array, (here - far) % ways * hop, a...]
  transfers between devices with their start and end apart: 2 -> 4, of which waited for: 2 -> 4; matrix products, arithmetic and copies ran while one was open for 5% -> 5% of each run, Pallas kernels for 0% -> 0%
where the time goes in v1:
time: 121 us
  waiting for transfers between devices  63.8 us (53%)
  blocking collectives  22.5 us (19%)
  between operations  14.2 us (12%)
  matrix products  12.9 us (11%)
  local copies, waits for them, and re-layouts  6.59 us (5%)
    psum x1, waiting for transfers between devices, shards(): summed_main, summed_check = lax.psum((product_main, product_check), 'row')  49.1 us
    psum x1, blocking collectives, shards(): summed_main, summed_check = lax.psum((product_main, product_check), 'row')  22.5 us
    ppermute x3, waiting for transfers between devices, gather_around(): lax.ppermute(array, axis, [(d, (d + 1) % ways) for d in range(ways)])  14.7 us
    dot_general x7, matrix products, matmul(): jnp.dot(left, right, precision=lax.Precision.HIGHEST, preferred_element_t...  12.9 us
    dynamic_update_slice x3, local copies, waits for them, and re-layouts, gather_around(): lax.dynamic_update_slice_in_dim(full, array, (here - far) % ways * hop, a...  2.92 us
  transfers between devices with their start and end apart: 4, of which 4 were waited for; matrix products, arithmetic and copies ran while one was open for 5% of the time, Pallas kernels for 0%

profile of v1, /device:TPU:0, one launch (start us, length us, event | category | flops | bytes accessed | tf_op | source)
XLA Modules:
  0.0 120.7 jit_solution(15927187103712420179)
XLA Ops:
  7.2 0.0 copy-start
  7.2 0.0 copy-start.4
  7.2 0.0 all-reduce.3.cloned.1.call-start
  7.2 0.5 collective-permute-start
  7.8 6.2 %collective-permute-done = f32[1024,64]{0,1:T(8,128)S(1)} collective-permute-done((f32[1024,64]{0,1:T(8,128)}, f32[1024,64]{0,1:T(8,128)S(1)}, u32[]{:S(2)}, u32[]{:S(2)}) %collective-permute-start) | collective-permute-done | bytes 262176 | tf_op jit(solution)/shard_map/ppermute | solution.py:14
  14.0 0.0 collective-permute-start.1
  14.0 0.1 broadcast_in_dim.3
  14.1 0.0 copy-start.1
  14.2 1.1 constant_dynamic-update-slice_fusion.3
  15.3 4.6 %collective-permute-done.1 = f32[1024,64]{0,1:T(8,128)} collective-permute-done((f32[1024,64]{0,1:T(8,128)S(1)}, f32[1024,64]{0,1:T(8,128)}, u32[]{:S(2)}, u32[]{:S(2)}) %collective-permute-start.1) | collective-permute-done | bytes 262176 | tf_op jit(solution)/shard_map/ppermute | solution.py:14
  19.9 0.0 collective-permute-start.2
  20.0 0.0 copy-done.3
  20.0 0.2 copy.8
  20.2 1.0 constant_dynamic-update-slice_fusion.2
  21.2 1.0 constant_dynamic-update-slice_fusion.1
  22.2 3.8 %collective-permute-done.2 = f32[1024,64]{0,1:T(8,128)} collective-permute-done((f32[1024,64]{0,1:T(8,128)}, f32[1024,64]{0,1:T(8,128)}, u32[]{:S(2)}, u32[]{:S(2)}) %collective-permute-start.2) | collective-permute-done | bytes 262176 | tf_op jit(solution)/shard_map/ppermute | solution.py:14
  26.0 1.0 constant_dynamic-update-slice_fusion
  27.0 3.4 %fusion = f32[256,386]{0,1:T(8,128)S(1)} fusion(f32[1024,256]{0,1:T(8,128)S(1)} %constant_dynamic-update-slice_fusion, f32[1024,2]{1,0:T(8,128)S(1)} %copy.8, f32[1024,384]{1,0:T(8,128)S(1)} %copy-done.1), kind=kOutput, calls=%fused_computation | convolution fusion | flops 1214646272 | bytes 3024896 | tf_op jit(solution)/shard_map/dot_general | solution.py:20
  30.4 0.0 copy-start.2
  30.5 0.7 copy-done.2
  31.2 0.8 slice.8
  32.0 0.7 slice.9
  32.7 0.0 all-reduce.3.cloned.1.call-update
  32.7 0.9 fusion.4
  33.6 22.5 %psum.15 = f32[256,2]{0,1:T(2,128)S(1)} all-reduce(f32[256,2]{0,1:T(2,128)S(1)} %slice.9), channel_id=1, replica_groups=mesh['row'=8,'col'=4] {'row'}, use_global_device_ids=true, to_apply=%region_1.2 | all-reduce | flops 512 | bytes 4096 | tf_op jit(solution)/shard_map/psum | solution.py:30
  56.1 0.2 fusion.9
  56.3 1.3 %convolution_subtract_fusion.1 = f32[1024,2]{0,1:T(2,128)} fusion(f32[1024,2]{0,1:T(2,128)S(1)} %copy-done.4, f32[1024,256]{0,1:T(8,128)S(1)} %constant_dynamic-update-slice_fusion, f32[2,256]{1,0:T(2,128)S(1)} %fusion.9), kind=kOutput, calls=%fused_computation.5 | convolution fusion | flops 6293504 | bytes 1067008 | tf_op jit(solution)/shard_map/dot_general | solution.py:20
  57.6 49.1 %all-reduce.3.cloned.1.call-done = f32[256,384]{0,1:T(8,128)} async-done(((f32[256,384]{0,1:T(8,128)}), f32[256,384]{0,1:T(8,128)}) %all-reduce.3.cloned.1.call-update) | async-done | bytes 393232 | tf_op jit(solution)/shard_map/psum | solution.py:30
  106.7 1.5 %fusion.8 = f32[384,256]{1,0:T(8,128)S(1)} fusion(f32[256,384]{0,1:T(8,128)} %all-reduce.3.cloned.1.call-done, f32[256,256]{1,0:T(8,128)S(1)} %copy-done), kind=kOutput, calls=%fused_computation.16 | convolution fusion | flops 301989888 | bytes 1048576 | tf_op jit(solution)/shard_map/dot_general | solution.py:20
  108.2 0.0 copy-start.5
  108.2 4.6 %convolution_subtract_fusion = f32[1024,384]{1,0:T(8,128)} fusion(f32[1024,384]{1,0:T(8,128)S(1)} %copy-done.1, f32[1024,256]{0,1:T(8,128)S(1)} %constant_dynamic-update-slice_fusion, f32[384,256]{1,0:T(8,128)S(1)} %fusion.8), kind=kOutput, calls=%fused_computation.4 | convolution fusion | flops 1208352768 | bytes 4587520 | tf_op jit(solution)/shard_map/dot_general | solution.py:20
  112.8 1.0 convolution_subtract_fusion.2
  (6 shorter events, 0.0 us)
Async XLA Ops:
  7.2 48.9 %copy-start = (f32[256,256]{1,0:T(8,128)S(1)}, f32[256,256]{1,0:T(8,128)}, u32[]{:S(2)}) copy-start(f32[256,256]{1,0:T(8,128)} %param.7) | copy-start | bytes 786436
  7.2 12.8 %copy-start.4 = (f32[1024,2]{0,1:T(2,128)S(1)}, f32[1024,2]{0,1:T(2,128)}, u32[]{:S(2)}) copy-start(f32[1024,2]{0,1:T(2,128)} %param.8) | copy-start | bytes 24580
  7.2 99.5 %all-reduce.3.cloned.1.call-start = ((), (), s32[]{:S(2)}) async-start(), calls=%async_computation | async-start | bytes 786432 | tf_op jit(solution)/shard_map/psum | solution.py:30
  7.2 6.8 %collective-permute-start = (f32[1024,64]{0,1:T(8,128)}, f32[1024,64]{0,1:T(8,128)S(1)}, u32[]{:S(2)}, u32[]{:S(2)}) collective-permute-start(f32[1024,64]{0,1:T(8,128)} %param.6), channel_id=1, source_target_pairs={{0,1},{1,2},{2,3},{3,0},{4,5},{5,6},{6,7},{7,4},{8,9},{9,10},{10,1... | collective-permute-start | bytes 786440 | tf_op jit(solution)/shard_map/ppermute | solution.py:14
  14.0 6.0 %copy-start.3 = (f32[1024,64]{0,1:T(8,128)}, f32[1024,64]{0,1:T(8,128)S(1)}, u32[]{:S(2)}) copy-start(f32[1024,64]{0,1:T(8,128)S(1)} %collective-permute-done) | copy-start | bytes 786436
  14.0 5.9 %collective-permute-start.1 = (f32[1024,64]{0,1:T(8,128)S(1)}, f32[1024,64]{0,1:T(8,128)}, u32[]{:S(2)}, u32[]{:S(2)}) collective-permute-start(f32[1024,64]{0,1:T(8,128)S(1)} %collective-permute-done), channel_id=1, source_target_pairs={{0,1},{1,2},{2,3},{3,0},{4,5},{5,6},{6,7},{7,4},{8,9},{9,10},{10,1... | collective-permute-start | bytes 786440 | tf_op jit(solution)/shard_map/ppermute | solution.py:14
  14.1 12.8 %copy-start.1 = (f32[1024,384]{1,0:T(8,128)S(1)}, f32[1024,384]{1,0:T(8,128)}, u32[]{:S(2)}) copy-start(f32[1024,384]{1,0:T(8,128)} %param.5) | copy-start | bytes 4718596
  19.9 6.1 %collective-permute-start.2 = (f32[1024,64]{0,1:T(8,128)}, f32[1024,64]{0,1:T(8,128)}, u32[]{:S(2)}, u32[]{:S(2)}) collective-permute-start(f32[1024,64]{0,1:T(8,128)} %collective-permute-done.1), channel_id=1, source_target_pairs={{0,1},{1,2},{2,3},{3,0},{4,5},{5,6},{6,7},{7,4},{8,9},{9,10},{10,1... | collective-permute-start | bytes 786440 | tf_op jit(solution)/shard_map/ppermute | solution.py:14
  30.4 0.8 copy-start.2
  108.2 4.6 %copy-start.5 = (f32[2,384]{1,0:T(2,128)S(1)}, f32[2,384]{1,0:T(2,128)}, u32[]{:S(2)}) copy-start(f32[2,384]{1,0:T(2,128)} %param.9) | copy-start | bytes 9220
Sparse Core Ops, SparseCore 0:
  32.8 73.8 all-reduce.2
